TPU v7x, 32 devices: a whole 2x2x4 slice. The times are simulated.
32 devices in a mesh: patch: 2 (over x), row: 4 (over y, core), col: 4 (over z).
Axes of the slice: x: 2, y: 2, z: 4, core: 2. Of those that a mesh axis runs over, the one named last changes fastest.
Arguments:
- sky_cube: float32 [512, 128, 512], P(None, ('patch', 'row'), 'col'), parts along dimension 1, may hold values from -40 to 140
- beam_taps: float32 [512, 33], replicated, may hold values from 0 to 0.2
Outputs:
- cleaned_cube: float32 [512, 128, 512], P(None, ('patch', 'row'), 'col'), parts along dimension 1
There are 2 independent parts, one for each index of `patch`. A program takes and returns all parts, laid end to end along the dimension named above; an argument that names none is the same for every part. Nothing has to cross between parts.
All inputs are finite; a program needn't handle non-finite values.
Results may differ from a plain program's by a relative error of at most 0.00085.
Values sent between devices are 32-bit elements; how exact they have to be, the bound alone decides.
No kernel may reach another device: no remote copies, remote signals or barrier semaphores. Data moves between devices by JAX's collectives and lax.ppermute only.
A program may use at most 64 MiB of HBM per device.

v0:
```python
import jax
import jax.numpy as jnp
from jax import lax
from jax.sharding import PartitionSpec as P

MODES = 4
SWEEPS = 3


def padded(array, sides, width):
    for axis, dim in sides:
        peers, length = (lax.axis_size(axis), array.shape[dim])
        up = [(i, (i + 1) % peers) for i in range(peers - 1)]
        down = [(j, i) for i, j in up]
        last = lax.slice_in_dim(array, length - width, length, axis=dim)
        leading = lax.slice_in_dim(array, 0, width, axis=dim)
        before = lax.ppermute(last, axis, up)
        after = lax.ppermute(leading, axis, down)
        array = jnp.concatenate([before, array, after], axis=dim)
    return array


def convolve(padded_field, beam_taps, axis_dim, out_width):
    result = None
    for offset in range(beam_taps.shape[1]):
        piece = lax.slice_in_dim(padded_field, offset, offset + out_width, axis=axis_dim)
        term = beam_taps[:, offset][:, None, None] * piece
        result = term if result is None else result + term
    return result


def orthonormalize(block):
    length = block.shape[0]
    columns = []
    for index in range(block.shape[1]):
        vector = block[:, index]
        for repeat in range(2):
            for earlier in columns:
                vector = vector - jnp.sum(earlier * vector) * earlier
        scale_mean = jnp.mean(vector * vector) + 1e-06
        vector = vector / jnp.sqrt(scale_mean) / jnp.sqrt(jnp.float32(length))
        columns.append(vector)
    return jnp.stack(columns, axis=1)


def leading_modes(gram_matrix, channels):
    scaled_gram = gram_matrix * (channels / jnp.trace(gram_matrix))
    channel_pos = jnp.arange(channels).astype(jnp.float32)
    mode_index = jnp.arange(MODES).astype(jnp.float32)
    cosine_basis = jnp.cos(jnp.pi * mode_index[None, :] * (channel_pos[:, None] + 0.5) / channels)
    basis = orthonormalize(cosine_basis)
    for sweep in range(SWEEPS):
        basis = orthonormalize(
            jnp.dot(
                scaled_gram,
                basis,
                precision=lax.Precision.HIGHEST,
                preferred_element_type=jnp.float32,
            )
        )
    return basis


def per_device(sky_cube, beam_taps):
    margin = beam_taps.shape[1] // 2
    channels, tile_rows, tile_cols = sky_cube.shape
    extended = padded(sky_cube, (("col", 2),), margin)
    smoothed = convolve(extended, beam_taps, 2, tile_cols)
    extended_rows = padded(smoothed, (("row", 1),), margin)
    beamed = convolve(extended_rows, beam_taps, 1, tile_rows)
    flattened = beamed.reshape(channels, tile_rows * tile_cols)
    partial_gram = jnp.dot(
        flattened, flattened.T, precision=lax.Precision.HIGHEST, preferred_element_type=jnp.float32
    )
    gram_matrix = lax.psum(partial_gram, ("row", "col"))
    mode_spectra = leading_modes(gram_matrix, channels)
    coefficients = jnp.dot(
        mode_spectra.T,
        flattened,
        precision=lax.Precision.HIGHEST,
        preferred_element_type=jnp.float32,
    )
    cleaned = flattened - jnp.dot(
        mode_spectra,
        coefficients,
        precision=lax.Precision.HIGHEST,
        preferred_element_type=jnp.float32,
    )
    return cleaned.reshape(channels, tile_rows, tile_cols)


def solution(mesh):
    placed = (P(None, ("patch", "row"), "col"), P())
    return jax.shard_map(
        per_device,
        mesh=mesh,
        in_specs=placed,
        out_specs=P(None, ("patch", "row"), "col"),
        check_vma=False,
    )
```

profile of v0, /device:TPU:0, one launch (start us, length us, event | category | flops | bytes accessed | tf_op | source)
XLA Modules:
  0.0 529.3 jit_solution(5304933710967582449)
XLA Ops:
  6.5 7.9 %fusion.232 = (f32[512,16,16]{2,1,0:T(8,128)}, f32[512,16,16]{2,1,0:T(8,128)}) fusion(f32[512,16,128]{2,1,0:T(8,128)} %param.2), kind=kLoop, calls=%fused_computation.501 | loop fusion | bytes 2097152 | tf_op jit(solution)/shard_map/slice | solution.py:15
  14.5 2.8 copy.12
  17.3 1.3 collective-permute-start.1
  18.6 2.8 copy.11
  21.4 5.6 %collective-permute-start = (f32[512,16,16]{0,2,1:T(8,128)S(1)}, f32[512,16,16]{0,2,1:T(8,128)S(1)}, u32[]{:S(2)}, u32[]{:S(2)}) collective-permute-start(f32[512,16,16]{0,2,1:T(8,128)S(1)} %copy.11), channel_id=1, source_target_pairs={{0,1},{1,2},{2,3},{4,5},{5,6},{6,7},{8,9},{9,10},{10,11},{12,13},{... | collective-permute-start | bytes 1572872 | tf_op jit(solution)/shard_map/ppermute | solution.py:17
  27.1 7.1 %collective-permute-done.1 = f32[512,16,16]{0,2,1:T(8,128)S(1)} collective-permute-done((f32[512,16,16]{0,2,1:T(8,128)S(1)}, f32[512,16,16]{0,2,1:T(8,128)S(1)}, u32[]{:S(2)}, u32[]{:S(2)}) %collective-permute-start.1) | collective-permute-done | bytes 524320 | tf_op jit(solution)/shard_map/ppermute | solution.py:18
  34.2 3.6 copy.8
  38.2 3.7 copy.6
  41.8 124.4 %fusion.91 = f32[512,16,128]{2,1,0:T(8,128)} fusion(f32[512,16,128]{2,1,0:T(8,128)} %param.2, f32[512,16,16]{2,1,0:T(8,128)} %copy.8, f32[512,16,16]{2,1,0:T(8,128)} %copy.6, f32[512]{0:T(512)S(1)} %bitcast.136, f32[512]{0:T(512)S(1)} %bitcast.138, f32[512]{0:T(512)S(1)} %bitcast.142, f32[512]{0:T(512)S(1)} %bitcast.144, f32[512]{0:T(512)S(1)} %bitcast.146, ...), kind=kLoop, calls=%fused_computation.207 | loop fusion | flops 101711872 | bytes 9504768 | tf_op jit(solution)/shard_map/add | solution.py:28
  166.3 1.3 collective-permute-start.3
  167.6 5.0 collective-permute-start.2
  187.5 114.2 %fusion.4 = f32[512,16,128]{2,1,0:T(8,128)S(1)} fusion(f32[512,16,128]{2,1,0:T(8,128)} %fusion.91, f32[512,16,128]{2,1,0:T(8,128)} %collective-permute-done.3, f32[512,16,128]{2,1,0:T(8,128)} %collective-permute-done.2, f32[512]{0:T(512)S(1)} %bitcast.137, f32[512]{0:T(512)S(1)} %bitcast.139, f32[512]{0:T(512)S(1)} %bitcast.143, f32[512]{0:T(512)S(1)} %bitcast.145, ...), kind=kLoop, calls=%fused_computation.120 | loop fusion | flops 99614720 | bytes 16844800 | tf_op jit(solution)/shard_map/add | solution.py:28
  301.7 2.0 copy-done
  303.7 10.8 %fusion.190 = f32[512,512]{1,0:T(8,128)} fusion(f32[512,16,128]{2,1,0:T(8,128)S(1)} %fusion.4), kind=kOutput, calls=%fused_computation.311 | convolution fusion | flops 6442450944 | bytes 5242880 | tf_op jit(solution)/shard_map/dot_general | solution.py:72
  318.3 123.3 %all-reduce.2.cloned.1.call-done = f32[512,512]{1,0:T(8,128)} async-done(((f32[512,512]{1,0:T(8,128)}), f32[512,512]{1,0:T(8,128)}) %all-reduce.2.cloned.1.call-update) | async-done | bytes 1048592 | tf_op jit(solution)/shard_map/psum | solution.py:75
  441.5 2.1 select_reduce_fusion
  444.3 2.2 fusion.197
  446.6 0.7 multiply_reduce_fusion.47
  452.8 0.7 multiply_reduce_fusion.42
  456.1 0.7 multiply_reduce_fusion.37
  459.3 0.7 multiply_reduce_fusion.36
  460.7 0.7 multiply_reduce_fusion.35
  463.5 0.7 multiply_reduce_fusion.33
  464.9 0.7 multiply_reduce_fusion.32
  466.3 2.2 fusion.195
  468.5 0.7 multiply_reduce_fusion.31
  474.8 0.7 multiply_reduce_fusion.26
  478.1 0.7 multiply_reduce_fusion.21
  481.3 0.7 multiply_reduce_fusion.20
  482.7 0.7 multiply_reduce_fusion.19
  485.5 0.7 multiply_reduce_fusion.17
  486.8 0.7 multiply_reduce_fusion.16
  488.3 1.0 fusion.193
  489.3 0.7 multiply_reduce_fusion.15
  490.8 0.7 multiply_reduce_fusion.14
  492.2 0.7 multiply_reduce_fusion.11
  494.1 0.7 multiply_reduce_fusion.12
  495.6 0.7 multiply_reduce_fusion.10
  497.0 0.7 multiply_reduce_fusion.6
  498.9 0.7 multiply_reduce_fusion.5
  502.1 0.7 multiply_reduce_fusion.4
  503.5 0.7 multiply_reduce_fusion.3
  504.9 0.7 multiply_reduce_fusion.2
  506.2 0.7 multiply_reduce_fusion.1
  507.6 0.7 multiply_reduce_fusion
  509.1 5.7 %fusion.180 = f32[4,2048]{1,0:T(4,128)S(1)} fusion(f32[64,8,16,128]{3,2,1,0:T(8,128)} %bitcast.86, f32[512,1]{0,1:T(1,128)S(1)} %divide_multiply_fusion, f32[512,1]{0,1:T(1,128)S(1)} %get-tuple-element.31, f32[512,1]{0,1:T(1,128)S(1)} %get-tuple-element.29, f32[512,1]{0,1:T(1,128)S(1)} %get-tuple-element.46), kind=kOutput, calls=%fused_computation.297 | convolution fusion | flops 50337792 | bytes 4235264 | tf_op jit(solution)/shard_map/dot_general | solution.py:77
  514.8 4.7 fusion.182
  519.5 2.9 copy.14
  (74 shorter events, 17.6 us)
Async XLA Ops:
  6.5 435.0 %all-reduce.2.cloned.1.call-start = ((), (), s32[]{:S(2)}) async-start(), calls=%async_computation | async-start | bytes 2097152 | tf_op jit(solution)/shard_map/psum | solution.py:75
  14.5 12.6 %copy-start.3 = (f32[512,33]{0,1:T(8,128)S(1)}, f32[512,33]{0,1:T(8,128)}, u32[]{:S(2)}) copy-start(f32[512,33]{0,1:T(8,128)} %param.3) | copy-start | bytes 202756
  17.3 16.9 %collective-permute-start.1 = (f32[512,16,16]{0,2,1:T(8,128)S(1)}, f32[512,16,16]{0,2,1:T(8,128)S(1)}, u32[]{:S(2)}, u32[]{:S(2)}) collective-permute-start(f32[512,16,16]{0,2,1:T(8,128)S(1)} %copy.12), channel_id=1, source_target_pairs={{1,0},{2,1},{3,2},{5,4},{6,5},{7,6},{9,8},{10,9},{11,10},{13,12},{... | collective-permute-start | bytes 1572872 | tf_op jit(solution)/shard_map/ppermute | solution.py:18
  21.4 16.8 %collective-permute-start = (f32[512,16,16]{0,2,1:T(8,128)S(1)}, f32[512,16,16]{0,2,1:T(8,128)S(1)}, u32[]{:S(2)}, u32[]{:S(2)}) collective-permute-start(f32[512,16,16]{0,2,1:T(8,128)S(1)} %copy.11), channel_id=1, source_target_pairs={{0,1},{1,2},{2,3},{4,5},{5,6},{6,7},{8,9},{9,10},{10,11},{12,13},{... | collective-permute-start | bytes 1572872 | tf_op jit(solution)/shard_map/ppermute | solution.py:17
  166.3 21.2 %collective-permute-start.3 = (f32[512,16,128]{2,1,0:T(8,128)}, f32[512,16,128]{2,1,0:T(8,128)}, u32[]{:S(2)}, u32[]{:S(2)}) collective-permute-start(f32[512,16,128]{2,1,0:T(8,128)} %fusion.91), channel_id=1, source_target_pairs={{4,0},{8,4},{12,8},{5,1},{9,5},{13,9},{6,2},{10,6},{14,10},{7,3},{... | collective-permute-start | bytes 12582920 | tf_op jit(solution)/shard_map/ppermute | solution.py:18
  167.6 19.9 %collective-permute-start.2 = (f32[512,16,128]{2,1,0:T(8,128)}, f32[512,16,128]{2,1,0:T(8,128)}, u32[]{:S(2)}, u32[]{:S(2)}) collective-permute-start(f32[512,16,128]{2,1,0:T(8,128)} %fusion.91), channel_id=1, source_target_pairs={{0,4},{4,8},{8,12},{1,5},{5,9},{9,13},{2,6},{6,10},{10,14},{3,7},{... | collective-permute-start | bytes 12582920 | tf_op jit(solution)/shard_map/ppermute | solution.py:17
  301.7 2.0 copy-start
  441.5 46.8 %copy-start.2 = (f32[512,512]{1,0:T(8,128)S(1)}, f32[512,512]{1,0:T(8,128)}, u32[]{:S(2)}) copy-start(f32[512,512]{1,0:T(8,128)} %all-reduce.2.cloned.1.call-done) | copy-start | bytes 3145732
  509.1 5.7 %copy-start.1 = (f32[512,16,128]{2,1,0:T(8,128)S(1)}, f32[512,16,128]{2,1,0:T(8,128)}, u32[]{:S(2)}) copy-start(f32[512,16,128]{2,1,0:T(8,128)} %copy-done) | copy-start | bytes 12582916
Sparse Core Ops, SparseCore 0:
  314.6 126.8 all-reduce.1
where the time goes:
time: 530 us; the launch traced here: 529 us
  other arithmetic  276 us (52%)
  waiting for transfers between devices  131 us (25%)
  between operations  57.1 us (11%)
  matrix products  26.6 us (5%)
  local copies, waits for them, and re-layouts  25.8 us (5%)
  starting transfers between devices  13.2 us (2%)
    add x2, other arithmetic, convolve(): result = term if result is None else result + term  239 us
    psum x1, waiting for transfers between devices, per_device(): gram_matrix = lax.psum(partial_gram, ('row', 'col'))  123 us
    reduce_sum x36, other arithmetic, orthonormalize(): vector = vector - jnp.sum(earlier * vector) * earlier  24 us
    dot_general x1, matrix products, per_device(): jnp.dot(flattened, flattened.T, precision=lax.Precision.HIGHEST, preferre...  10.8 us
    ppermute x2, starting transfers between devices, padded(): before = lax.ppermute(last, axis, up)  10.6 us
  transfers between devices with their start and end apart: 5, of which 3 were waited for; matrix products, arithmetic and copies ran while one was open for 3% of the time, Pallas kernels for 0%

commit v1 on v0

--- a/solution.py
+++ b/solution.py
@@ -2,9 +2,14 @@
 import jax.numpy as jnp
 from jax import lax
 from jax.sharding import PartitionSpec as P
+from jax.lax import all_gather
 
 MODES = 4
 SWEEPS = 3
+
+
+def manage_flows_on(my_tile):
+    return jnp.sum(all_gather(my_tile, axis_name=("row", "col")), axis=0)
 
 
 def padded(array, sides, width):
@@ -72,7 +77,7 @@
     partial_gram = jnp.dot(
         flattened, flattened.T, precision=lax.Precision.HIGHEST, preferred_element_type=jnp.float32
     )
-    gram_matrix = lax.psum(partial_gram, ("row", "col"))
+    gram_matrix = manage_flows_on(partial_gram)
     mode_spectra = leading_modes(gram_matrix, channels)
     coefficients = jnp.dot(
         mode_spectra.T,

time: 530 us -> 477 us (0.900)
  other arithmetic: 276 us -> 193 us
  waiting for transfers between devices: 131 us -> 165 us
    all_gather x0 -> x1, waiting for transfers between devices: none -> 151 us  [manage_flows_on(): return jnp.sum(all_gather(my_tile, axis_name=('row', 'col')), axis=0)]
    psum x1 -> x0, waiting for transfers between devices: 123 us -> none  [per_device(): gram_matrix = lax.psum(partial_gram, ('row', 'col'))]
    add x2, other arithmetic: 239 us -> 149 us  [convolve(): result = term if result is None else result + term]
    reduce_sum x0 -> x1, other arithmetic: none -> 7.91 us  [manage_flows_on(): return jnp.sum(all_gather(my_tile, axis_name=('row', 'col')), axis=0)]
  transfers between devices with their start and end apart: 5 -> 5, of which waited for: 3 -> 5; matrix products, arithmetic and copies ran while one was open for 3% -> 3% of each run, Pallas kernels for 0% -> 0%
where the time goes in v1:
time: 477 us; the launch traced here: 476 us
  other arithmetic  193 us (40%)
  waiting for transfers between devices  165 us (35%)
  between operations  56.5 us (12%)
  local copies, waits for them, and re-layouts  25.8 us (5%)
  matrix products  24.2 us (5%)
  starting transfers between devices  11.5 us (2%)
    all_gather x1, waiting for transfers between devices, manage_flows_on(): return jnp.sum(all_gather(my_tile, axis_name=('row', 'col')), axis=0)  151 us
    add x2, other arithmetic, convolve(): result = term if result is None else result + term  149 us
    reduce_sum x36, other arithmetic, orthonormalize(): vector = vector - jnp.sum(earlier * vector) * earlier  24.2 us
    ppermute x2, waiting for transfers between devices, padded(): after = lax.ppermute(leading, axis, down)  11.5 us
    dot_general x1, matrix products, per_device(): jnp.dot(flattened, flattened.T, precision=lax.Precision.HIGHEST, preferre...  10.7 us
    unnamed x9, local copies, waits for them, and re-layouts  10.6 us
    reduce_sum x16, other arithmetic, orthonormalize(): scale_mean = jnp.mean(vector * vector) + 1e-06  10.6 us
  transfers between devices with their start and end apart: 5, of which 5 were waited for; matrix products, arithmetic and copies ran while one was open for 3% of the time, Pallas kernels for 0%

profile of v1, /device:TPU:0, one launch (start us, length us, event | category | flops | bytes accessed | tf_op | source)
XLA Modules:
  0.0 476.0 jit_solution(13205104775381721448)
XLA Ops:
  6.5 7.9 %fusion.232 = (f32[512,16,16]{2,1,0:T(8,128)}, f32[512,16,16]{2,1,0:T(8,128)}) fusion(f32[512,16,128]{2,1,0:T(8,128)} %param.2), kind=kLoop, calls=%fused_computation.501 | loop fusion | bytes 2097152 | tf_op jit(solution)/shard_map/slice | solution.py:20
  14.5 2.8 copy.18
  17.3 1.3 collective-permute-start.1
  18.6 2.8 copy.17
  21.4 5.6 %collective-permute-start = (f32[512,16,16]{0,2,1:T(8,128)S(1)}, f32[512,16,16]{0,2,1:T(8,128)S(1)}, u32[]{:S(2)}, u32[]{:S(2)}) collective-permute-start(f32[512,16,16]{0,2,1:T(8,128)S(1)} %copy.17), channel_id=1, source_target_pairs={{0,1},{1,2},{2,3},{4,5},{5,6},{6,7},{8,9},{9,10},{10,11},{12,13},{... | collective-permute-start | bytes 1572872 | tf_op jit(solution)/shard_map/ppermute | solution.py:22
  27.1 7.1 %collective-permute-done.1 = f32[512,16,16]{0,2,1:T(8,128)S(1)} collective-permute-done((f32[512,16,16]{0,2,1:T(8,128)S(1)}, f32[512,16,16]{0,2,1:T(8,128)S(1)}, u32[]{:S(2)}, u32[]{:S(2)}) %collective-permute-start.1) | collective-permute-done | bytes 524320 | tf_op jit(solution)/shard_map/ppermute | solution.py:23
  34.2 3.6 copy.14
  38.2 3.6 copy.12
  41.8 120.8 %fusion.91 = f32[512,16,128]{2,1,0:T(8,128)S(1)} fusion(f32[512,16,128]{2,1,0:T(8,128)} %param.2, f32[512,16,16]{2,1,0:T(8,128)} %copy.14, f32[512,16,16]{2,1,0:T(8,128)} %copy.12, f32[512]{0:T(512)S(1)} %bitcast.138, f32[512]{0:T(512)S(1)} %bitcast.140, f32[512]{0:T(512)S(1)} %bitcast.144, f32[512]{0:T(512)S(1)} %bitcast.146, f32[512]{0:T(512)S(1)} %bitcast.148, ...), kind=kLoop, calls=%fused_computation.207 | loop fusion | flops 101711872 | bytes 9504768 | tf_op jit(solution)/shard_map/add | solution.py:33
  162.6 1.3 collective-permute-start.3
  163.9 3.3 collective-permute-start.2
  167.2 4.4 collective-permute-done.3
  171.7 2.1 collective-permute-done.2
  173.7 28.0 %fusion.4 = f32[512,16,128]{2,1,0:T(8,128)S(1)} fusion(f32[512,16,128]{2,1,0:T(8,128)S(1)} %fusion.91, f32[512,16,128]{2,1,0:T(8,128)S(1)} %collective-permute-done.3, f32[512,16,128]{2,1,0:T(8,128)S(1)} %collective-permute-done.2, f32[512]{0:T(512)S(1)} %bitcast.139, f32[512]{0:T(512)S(1)} %bitcast.141, f32[512]{0:T(512)S(1)} %bitcast.145, ...), kind=kLoop, calls=%fused_computation.120 | loop fusion | flops 99614720 | bytes 16844800 | tf_op jit(solution)/shard_map/add | solution.py:33
  201.7 2.0 copy-done
  203.7 10.7 %fusion.190 = f32[512,512]{1,0:T(8,128)} fusion(f32[512,16,128]{2,1,0:T(8,128)S(1)} %fusion.4), kind=kOutput, calls=%fused_computation.311 | convolution fusion | flops 6442450944 | bytes 5242880 | tf_op jit(solution)/shard_map/dot_general | solution.py:77
  223.4 0.7 multiply_reduce_fusion.53
  232.7 151.3 %all-gather.3.cloned.1.call-done = f32[8192,512]{1,0:T(8,128)} async-done(((f32[512,512]{1,0:T(8,128)}), f32[8192,512]{1,0:T(8,128)}) %all-gather.3.cloned.1.call-update) | async-done | bytes 16777232 | tf_op jit(solution)/shard_map/all_gather | solution.py:12
  384.1 7.9 %reduce_sum.595 = f32[512,512]{1,0:T(8,128)S(1)} reduce(f32[16,512,512]{2,1,0:T(8,128)} %bitcast.89, f32[]{:T(128)} %constant.44.clone.1), dimensions={0}, to_apply=%region_0.0 | reduce | flops 3932160 | bytes 17825796 | tf_op jit(solution)/shard_map/reduce_sum | solution.py:12
  392.0 0.8 select_reduce_fusion
  393.5 1.0 fusion.197
  394.5 0.7 multiply_reduce_fusion.47
  400.7 0.7 multiply_reduce_fusion.42
  404.1 0.7 multiply_reduce_fusion.37
  407.2 0.7 multiply_reduce_fusion.36
  408.6 0.7 multiply_reduce_fusion.35
  410.0 0.7 multiply_reduce_fusion.34
  411.4 0.7 multiply_reduce_fusion.33
  412.8 0.7 multiply_reduce_fusion.32
  414.2 1.2 fusion.195
  415.5 0.7 multiply_reduce_fusion.31
  421.7 0.7 multiply_reduce_fusion.26
  425.1 0.7 multiply_reduce_fusion.21
  428.2 0.7 multiply_reduce_fusion.20
  429.6 0.7 multiply_reduce_fusion.19
  432.4 0.7 multiply_reduce_fusion.17
  433.8 0.7 multiply_reduce_fusion.16
  435.2 1.0 fusion.193
  436.2 0.7 multiply_reduce_fusion.15
  442.5 0.7 multiply_reduce_fusion.10
  445.8 0.7 multiply_reduce_fusion.5
  449.0 0.7 multiply_reduce_fusion.4
  450.4 0.7 multiply_reduce_fusion.3
  453.2 0.7 multiply_reduce_fusion.1
  454.6 0.7 multiply_reduce_fusion
  456.0 5.5 %fusion.180 = f32[4,2048]{1,0:T(4,128)S(1)} fusion(f32[64,8,16,128]{3,2,1,0:T(8,128)} %bitcast.87, f32[512,1]{0,1:T(1,128)S(1)} %divide_multiply_fusion, f32[512,1]{0,1:T(1,128)S(1)} %get-tuple-element.31, f32[512,1]{0,1:T(1,128)S(1)} %get-tuple-element.29, f32[512,1]{0,1:T(1,128)S(1)} %get-tuple-element.46), kind=kOutput, calls=%fused_computation.297 | convolution fusion | flops 50337792 | bytes 4235264 | tf_op jit(solution)/shard_map/dot_general | solution.py:82
  461.5 4.7 fusion.182
  466.3 2.9 copy.20
  (73 shorter events, 19.8 us)
Async XLA Ops:
  6.5 377.5 %all-gather.3.cloned.1.call-start = ((), (), s32[]{:S(2)}) async-start(), calls=%async_computation | async-start | bytes 17825792 | tf_op jit(solution)/shard_map/all_gather | solution.py:12
  14.5 12.6 %copy-start.2 = (f32[512,33]{0,1:T(8,128)S(1)}, f32[512,33]{0,1:T(8,128)}, u32[]{:S(2)}) copy-start(f32[512,33]{0,1:T(8,128)} %param.3) | copy-start | bytes 202756
  17.3 16.9 %collective-permute-start.1 = (f32[512,16,16]{0,2,1:T(8,128)S(1)}, f32[512,16,16]{0,2,1:T(8,128)S(1)}, u32[]{:S(2)}, u32[]{:S(2)}) collective-permute-start(f32[512,16,16]{0,2,1:T(8,128)S(1)} %copy.18), channel_id=1, source_target_pairs={{1,0},{2,1},{3,2},{5,4},{6,5},{7,6},{9,8},{10,9},{11,10},{13,12},{... | collective-permute-start | bytes 1572872 | tf_op jit(solution)/shard_map/ppermute | solution.py:23
  21.4 16.8 %collective-permute-start = (f32[512,16,16]{0,2,1:T(8,128)S(1)}, f32[512,16,16]{0,2,1:T(8,128)S(1)}, u32[]{:S(2)}, u32[]{:S(2)}) collective-permute-start(f32[512,16,16]{0,2,1:T(8,128)S(1)} %copy.17), channel_id=1, source_target_pairs={{0,1},{1,2},{2,3},{4,5},{5,6},{6,7},{8,9},{9,10},{10,11},{12,13},{... | collective-permute-start | bytes 1572872 | tf_op jit(solution)/shard_map/ppermute | solution.py:22
  162.6 9.1 %collective-permute-start.3 = (f32[512,16,128]{2,1,0:T(8,128)S(1)}, f32[512,16,128]{2,1,0:T(8,128)S(1)}, u32[]{:S(2)}, u32[]{:S(2)}) collective-permute-start(f32[512,16,128]{2,1,0:T(8,128)S(1)} %fusion.91), channel_id=1, source_target_pairs={{4,0},{8,4},{12,8},{5,1},{9,5},{13,9},{6,2},{10,6},{14,10},{7,3},{... | collective-permute-start | bytes 12582920 | tf_op jit(solution)/shard_map/ppermute | solution.py:23
  163.9 9.8 %collective-permute-start.2 = (f32[512,16,128]{2,1,0:T(8,128)S(1)}, f32[512,16,128]{2,1,0:T(8,128)S(1)}, u32[]{:S(2)}, u32[]{:S(2)}) collective-permute-start(f32[512,16,128]{2,1,0:T(8,128)S(1)} %fusion.91), channel_id=1, source_target_pairs={{0,4},{4,8},{8,12},{1,5},{5,9},{9,13},{2,6},{6,10},{10,14},{3,7},{... | collective-permute-start | bytes 12582920 | tf_op jit(solution)/shard_map/ppermute | solution.py:22
  201.7 2.0 copy-start
  456.0 5.5 %copy-start.1 = (f32[512,16,128]{2,1,0:T(8,128)S(1)}, f32[512,16,128]{2,1,0:T(8,128)}, u32[]{:S(2)}) copy-start(f32[512,16,128]{2,1,0:T(8,128)} %copy-done) | copy-start | bytes 12582916
Sparse Core Ops, SparseCore 0:
  214.6 169.4 all-gather.2
